TPU v7x, 32 devices: a whole 2x2x4 slice. The times are simulated.
32 devices in a mesh: groups: 2 (over y), blk: 16 (over z, x, core).
Axes of the slice: x: 2, y: 2, z: 4, core: 2. Of those that a mesh axis runs over, the one named last changes fastest.
Arguments:
- query_hidden: bfloat16 [512, 32, 768], P(('groups', 'blk')), parts along dimension 0, may hold values from -6 to 6
- passage_hidden: bfloat16 [256, 180, 768], P(('groups', 'blk')), parts along dimension 0, may hold values from -6 to 6
- projection: bfloat16 [768, 128], replicated, may hold values from -0.21875 to 0.21875
- teacher_rows: float32 [512, 32], P(('groups', 'blk')), parts along dimension 0, may hold values from -12 to 12
- teacher_pos: int32 [512], P(('groups', 'blk')), parts along dimension 0, may hold values from 0 to 255, each once
- neg_count: int32 [512], P(('groups', 'blk')), parts along dimension 0, may hold values from 8 to 32
- pass_len: int32 [256], P(('groups', 'blk')), parts along dimension 0, may hold values from 19 to 180
Outputs:
- loss: float32 [512], P(('groups', 'blk')), parts along dimension 0
- grad_w: float32 [1536, 128], P(('groups', 'blk')), parts along dimension 0
There are 2 independent parts, one for each index of `groups`. A program takes and returns all parts, laid end to end along the dimension named above; an argument that names none is the same for every part. Nothing has to cross between parts.
Inputs may be any that keep to these rules, and one draw needn't show every extreme that they name: A permutation: the teacher scores of query q are stored as row teacher_pos[q] of teacher_rows.
All inputs are finite; a program needn't handle non-finite values.
Results may differ from a plain program's by a relative error of at most 0.0073.
Values may be sent and summed in bfloat16 or wider, within the bound.
A program may use at most 128 MiB of HBM per device.

v0:
```python
import jax
import jax.numpy as jnp
from jax import lax
from jax.sharding import PartitionSpec as P

CYCLE = 4
smoothing_heat_factor = 0.05
epsilon = 1e-06


def shifted(value, axis, steps):
    count = lax.axis_size(axis)
    pairs = [(source, (source + steps) % count) for source in range(count)]
    return lax.ppermute(value, axis, pairs)


def normalize(raw):
    length = jnp.sqrt(jnp.sum(raw * raw, axis=1, keepdims=True) + epsilon)
    return (raw / length, length)


def token_terms(query_flat, passage_flat, lengths):
    count = lengths.shape[0]
    token_affinity_table = lax.dot_general(
        query_flat, passage_flat, (((1,), (1,)), ((), ())), preferred_element_type=jnp.float32
    )
    token_affinity_table = token_affinity_table.reshape(query_flat.shape[0], count, -1)
    pairwise_dot_entries = (
        jnp.arange(token_affinity_table.shape[2], dtype=jnp.int32)[None, :] < lengths[:, None]
    )
    natural_power_entries = jnp.where(
        pairwise_dot_entries[None], jnp.exp(token_affinity_table / smoothing_heat_factor), 0.0
    )
    return (natural_power_entries, jnp.sum(natural_power_entries, axis=2))


def soft_scores(query_flat, passage_flat, lengths, query_matrix):
    natural_power_entries, power_totals_row = token_terms(query_flat, passage_flat, lengths)
    smooth_peak_values = smoothing_heat_factor * jnp.log(power_totals_row)
    return jnp.sum(smooth_peak_values.reshape(query_matrix, -1, lengths.shape[0]), axis=1)


def score_grads(query_flat, passage_flat, lengths, score_grad):
    natural_power_entries, power_totals_row = token_terms(query_flat, passage_flat, lengths)
    rows = query_flat.shape[0]
    query_matrix, count = score_grad.shape
    scale = (score_grad[:, None, :] / power_totals_row.reshape(query_matrix, -1, count)).reshape(
        rows, count
    )
    weights = (natural_power_entries * scale[:, :, None]).reshape(rows, -1).astype(jnp.bfloat16)
    query_grad = jnp.dot(weights, passage_flat, preferred_element_type=jnp.float32)
    passage_grad = lax.dot_general(
        weights, query_flat, (((0,), (0,)), ((), ())), preferred_element_type=jnp.float32
    )
    return (query_grad, passage_grad)


def kl_terms(student, teacher, counts):
    valid = jnp.arange(student.shape[1], dtype=jnp.int32)[None, :] < counts[:, None]
    student_exp = jnp.where(valid, jnp.exp(student), 0.0)
    student_total = jnp.sum(student_exp, axis=1, keepdims=True)
    teacher_exp = jnp.where(valid, jnp.exp(teacher), 0.0)
    teacher_total = jnp.sum(teacher_exp, axis=1, keepdims=True)
    student_prob = student_exp / student_total
    teacher_prob = teacher_exp / teacher_total
    gap = teacher - jnp.log(teacher_total) - (student - jnp.log(student_total))
    loss = jnp.sum(jnp.where(valid, teacher_prob * gap, 0.0), axis=1)
    return (loss, student_prob - teacher_prob)


def raw_grad(unit, length, grad):
    return ((grad - unit * jnp.sum(unit * grad, axis=1, keepdims=True)) / length).astype(
        jnp.bfloat16
    )


def per_device(
    query_hidden, passage_hidden, projection, teacher_rows, teacher_pos, neg_count, pass_len
):
    query_matrix = query_hidden.shape[0]
    query_tokens = query_hidden.shape[1]
    width = query_hidden.shape[2]
    passages = passage_hidden.shape[0]
    passage_tokens = passage_hidden.shape[1]
    query_flat = query_hidden.reshape(query_matrix * query_tokens, width)
    passage_flat = passage_hidden.reshape(passages * passage_tokens, width)
    query_unit, query_length = normalize(
        jnp.dot(query_flat, projection, preferred_element_type=jnp.float32)
    )
    passage_unit, passage_length = normalize(
        jnp.dot(passage_flat, projection, preferred_element_type=jnp.float32)
    )
    query_outgoing = query_unit.astype(jnp.bfloat16)
    passage_send = passage_unit.astype(jnp.bfloat16)
    stored = lax.all_gather(teacher_rows, "blk", axis=0, tiled=True)
    teacher = jnp.take(stored, teacher_pos, axis=0)
    score_parts = []
    held = []
    current = query_outgoing
    for offset in range(CYCLE):
        if offset > 0:
            current = shifted(current, "blk", 1)
        held.append(current)
        scored = soft_scores(current, passage_send, pass_len, query_matrix)
        if offset > 0:
            scored = shifted(scored, "blk", -offset)
        score_parts.append(scored)
    student = jnp.concatenate(score_parts, axis=1)
    loss, score_grad = kl_terms(student, teacher, neg_count)
    query_total = jnp.zeros(query_unit.shape, jnp.float32)
    passage_total = jnp.zeros(passage_unit.shape, jnp.float32)
    for offset in range(CYCLE):
        portion_derivative = score_grad[:, offset * passages : (offset + 1) * passages]
        if offset > 0:
            portion_derivative = shifted(portion_derivative, "blk", offset)
        query_part, passage_part = score_grads(
            held[offset], passage_send, pass_len, portion_derivative
        )
        passage_total = passage_total + passage_part
        if offset > 0:
            query_part = shifted(query_part, "blk", -offset)
        query_total = query_total + query_part
    query_raw = raw_grad(query_unit, query_length, query_total)
    document_unprojected = raw_grad(passage_unit, passage_length, passage_total)
    contract = (((0,), (0,)), ((), ()))
    term = lax.dot_general(query_flat, query_raw, contract, preferred_element_type=jnp.float32)
    grad_w = lax.psum_scatter(
        term
        + lax.dot_general(
            passage_flat, document_unprojected, contract, preferred_element_type=jnp.float32
        ),
        "blk",
        scatter_dimension=0,
        tiled=True,
    )
    return (loss, grad_w)


def solution(mesh):
    return jax.shard_map(
        per_device,
        mesh=mesh,
        in_specs=(
            P(("groups", "blk"), None, None),
            P(("groups", "blk"), None, None),
            P(),
            P(("groups", "blk"), None),
            P(("groups", "blk")),
            P(("groups", "blk")),
            P(("groups", "blk")),
        ),
        out_specs=(P(("groups", "blk")), P(("groups", "blk"), None)),
        check_vma=False,
    )
```

profile of v0, /device:TPU:0, one launch (start us, length us, event | category | flops | bytes accessed | tf_op | source)
XLA Modules:
  0.0 242.0 jit_solution(9073984573945769077)
XLA Ops:
  14.1 3.4 %copy.26 = bf16[8,180,768]{2,1,0:T(8,128)(2,1)} copy(bf16[8,180,768]{2,0,1:T(8,128)(2,1)} %param.8) | data formatting | bytes 4423680 | tf_op args[1]
  17.5 2.6 %reshape.162 = bf16[1440,768]{1,0:T(8,128)(2,1)S(1)} reshape(bf16[8,180,768]{2,1,0:T(8,128)(2,1)} %copy.26) | data formatting | bytes 4423680 | tf_op jit(solution)/shard_map/reshape | solution.py:86
  22.1 2.1 fusion
  24.5 3.1 %exp.40 = f32[512,8,180]{0,2,1:T(8,128)} reshape(f32[512,1440]{0,1:T(8,128)} %fusion) | data formatting | bytes 5898240 | tf_op jit(solution)/shard_map/exp | solution.py:32
  27.6 24.4 %all_gather.3 = f32[256,32]{1,0:T(8,128)} all-gather(f32[16,32]{1,0:T(8,128)S(1)} %copy-done.11), channel_id=1, replica_groups=mesh['groups'=2,'blk'=16] {'blk'}, dimensions={0}, use_global_device_ids=true | all-gather | bytes 34816 | tf_op jit(solution)/shard_map/all_gather | solution.py:95
  52.9 3.1 %fusion.1 = f32[512,1440]{0,1:T(8,128)} fusion(bf16[1440,128]{1,0:T(8,128)(2,1)S(1)} %fusion.16, bf16[512,128]{0,1:T(8,128)(2,1)} %collective-permute-done), kind=kOutput, calls=%fused_computation.6 | convolution fusion | flops 189480960 | bytes 3448832 | tf_op jit(solution)/shard_map/dot_general | solution.py:24
  55.9 3.1 %exp.42 = f32[512,8,180]{0,2,1:T(8,128)} reshape(f32[512,1440]{0,1:T(8,128)} %fusion.1) | data formatting | bytes 5898240 | tf_op jit(solution)/shard_map/exp | solution.py:32
  59.9 3.1 %fusion.2 = f32[512,1440]{0,1:T(8,128)} fusion(bf16[1440,128]{1,0:T(8,128)(2,1)S(1)} %fusion.16, bf16[512,128]{0,1:T(8,128)(2,1)} %collective-permute-done.2), kind=kOutput, calls=%fused_computation.7 | convolution fusion | flops 189480960 | bytes 3448832 | tf_op jit(solution)/shard_map/dot_general | solution.py:24
  63.0 3.2 %exp.44 = f32[512,8,180]{0,2,1:T(8,128)} reshape(f32[512,1440]{0,1:T(8,128)} %fusion.2) | data formatting | bytes 5898240 | tf_op jit(solution)/shard_map/exp | solution.py:32
  67.3 3.0 %fusion.3 = f32[512,1440]{0,1:T(8,128)} fusion(bf16[1440,128]{1,0:T(8,128)(2,1)S(1)} %fusion.16, bf16[512,128]{0,1:T(8,128)(2,1)} %collective-permute-done.4), kind=kOutput, calls=%fused_computation.8 | convolution fusion | flops 189480960 | bytes 3448832 | tf_op jit(solution)/shard_map/dot_general | solution.py:24
  70.4 3.1 %exp.46 = f32[512,8,180]{0,2,1:T(8,128)} reshape(f32[512,1440]{0,1:T(8,128)} %fusion.3) | data formatting | bytes 5898240 | tf_op jit(solution)/shard_map/exp | solution.py:32
  73.5 5.7 %select_reduce_fusion.3 = (f32[512,8]{0,1:T(8,128)}, f32[512,8]{0,1:T(8,128)S(1)}, f32[512,8]{0,1:T(8,128)S(1)}, f32[512,8]{0,1:T(8,128)S(1)}) fusion(f32[512,8,180]{0,2,1:T(8,128)} %exp.40, pred[8,180]{1,0:T(8,128)(4,1)} %iota_compare_fusion, f32[512,8,180]{0,2,1:T(8,128)} %exp.42, f32[512,8,180]{0,2,1:T(8,128)} %exp.44, f32[512,8,180]{0,2,1:T(8,128)} %exp.46), kind=kLoop, calls=%fused_computation.12 | loop fusion | flops 5881856 | bytes 11863456 | tf_op jit(solution)/shard_map/reduce_sum | solution.py:34
  89.8 3.4 %collective-permute-start.1 = (f32[16,8]{1,0:T(8,128)}, f32[16,8]{1,0:T(8,128)}, u32[]{:S(2)}, u32[]{:S(2)}) collective-permute-start(f32[16,8]{1,0:T(8,128)} %copy.27), channel_id=1, source_target_pairs={{0,15},{1,0},{2,1},{3,2},{4,3},{5,4},{6,5},{7,6},{8,7},{9,8},{10,9... | collective-permute-start | bytes 1544 | tf_op jit(solution)/shard_map/ppermute | solution.py:14
  110.4 3.5 %collective-permute-start.10 = (f32[16,8]{1,0:T(8,128)}, f32[16,8]{1,0:T(8,128)}, u32[]{:S(2)}, u32[]{:S(2)}) collective-permute-start(f32[16,8]{1,0:T(8,128)} %get-tuple-element.17), channel_id=1, source_target_pairs={{0,3},{1,4},{2,5},{3,6},{4,7},{5,8},{6,9},{7,10},{8,11},{9,12},{10... | collective-permute-start | bytes 1544 | tf_op jit(solution)/shard_map/ppermute | solution.py:14
  119.5 3.1 %mul.115 = f32[512,1440]{0,1:T(8,128)} reshape(f32[512,8,180]{0,2,1:T(8,128)} %mul.114) | data formatting | bytes 5898240 | tf_op jit(solution)/shard_map/mul | solution.py:50
  136.4 3.1 %mul.124 = f32[512,1440]{0,1:T(8,128)} reshape(f32[512,8,180]{0,2,1:T(8,128)} %mul.123) | data formatting | bytes 5898240 | tf_op jit(solution)/shard_map/mul | solution.py:50
  141.5 3.1 %mul.121 = f32[512,1440]{0,1:T(8,128)} reshape(f32[512,8,180]{0,2,1:T(8,128)} %mul.120) | data formatting | bytes 5898240 | tf_op jit(solution)/shard_map/mul | solution.py:50
  144.6 2.1 mul.117
  146.7 3.1 %mul.118 = f32[512,1440]{0,1:T(8,128)} reshape(f32[512,8,180]{0,2,1:T(8,128)} %mul.117) | data formatting | bytes 5898240 | tf_op jit(solution)/shard_map/mul | solution.py:50
  149.8 8.6 %multiply_convert_fusion = (bf16[512,1440]{0,1:T(8,128)(2,1)S(1)}, bf16[512,1440]{0,1:T(8,128)(2,1)S(1)}, bf16[512,1440]{0,1:T(8,128)(2,1)S(1)}, bf16[512,1440]{0,1:T(8,128)(2,1)S(1)}) fusion(f32[512,1440]{0,1:T(8,128)} %mul.124, f32[512,1440]{0,1:T(8,128)} %fusion.3, pred[1440]{0:T(1024)(128)(4,1)S(1)} %copy-done.12, f32[512,1440]{0,1:T(8,128)} %mul.118, ...), kind=kLoop, calls=%fused_computation.13 | loop fusion | flops 8847360 | bytes 29492640 | tf_op jit(solution)/shard_map/convert_element_type | solution.py:50
  159.7 4.8 %collective-permute-start.9 = (f32[512,128]{0,1:T(8,128)S(1)}, f32[512,128]{0,1:T(8,128)S(1)}, u32[]{:S(2)}, u32[]{:S(2)}) collective-permute-start(f32[512,128]{0,1:T(8,128)S(1)} %fusion.19), channel_id=1, source_target_pairs={{0,14},{1,15},{2,0},{3,1},{4,2},{5,3},{6,4},{7,5},{8,6},{9,7},{10,... | collective-permute-start | bytes 786440 | tf_op jit(solution)/shard_map/ppermute | solution.py:14
  171.2 3.2 %collective-permute-done.7 = f32[512,128]{0,1:T(8,128)S(1)} collective-permute-done((f32[512,128]{0,1:T(8,128)S(1)}, f32[512,128]{0,1:T(8,128)S(1)}, u32[]{:S(2)}, u32[]{:S(2)}) %collective-permute-start.7) | collective-permute-done | bytes 262176 | tf_op jit(solution)/shard_map/ppermute | solution.py:14
  174.5 2.8 %collective-permute-done.11 = f32[512,128]{0,1:T(8,128)S(1)} collective-permute-done((f32[512,128]{0,1:T(8,128)S(1)}, f32[512,128]{0,1:T(8,128)S(1)}, u32[]{:S(2)}, u32[]{:S(2)}) %collective-permute-start.11) | collective-permute-done | bytes 262176 | tf_op jit(solution)/shard_map/ppermute | solution.py:14
  179.0 56.2 %reduce-scatter.4.cloned.1.call-done = f32[48,128]{1,0:T(8,128)} async-done(((f32[768,128]{1,0:T(8,128)}), f32[48,128]{1,0:T(8,128)}) %reduce-scatter.4.cloned.1.call-update) | async-done | bytes 24592
  (114 shorter events, 70.6 us)
Async XLA Ops:
  7.2 1.1 copy-start
  7.2 228.0 %reduce-scatter.4.cloned.1.call-start = ((), (), s32[]{:S(2)}) async-start(), calls=%async_computation.1 | async-start | bytes 417792
  10.4 42.2 %collective-permute-start = (bf16[512,128]{0,1:T(8,128)(2,1)S(1)}, bf16[512,128]{0,1:T(8,128)(2,1)}, u32[]{:S(2)}, u32[]{:S(2)}) collective-permute-start(bf16[512,128]{0,1:T(8,128)(2,1)S(1)} %fusion.15), channel_id=1, source_target_pairs={{0,1},{1,2},{2,3},{3,4},{4,5},{5,6},{6,7},{7,8},{8,9},{9,10},{10,1... | collective-permute-start | bytes 393224 | tf_op jit(solution)/shard_map/ppermute | solution.py:14
  17.5 2.6 %copy-start.5 = (bf16[768,128]{1,0:T(8,128)(2,1)S(1)}, bf16[768,128]{1,0:T(8,128)(2,1)}, u32[]{:S(2)}) copy-start(bf16[768,128]{1,0:T(8,128)(2,1)} %param.9) | copy-start | bytes 589828
  21.0 3.3 %copy-start.13 = (s32[8]{0:T(128)S(1)}, s32[8]{0:T(128)}, u32[]{:S(2)}) copy-start(s32[8]{0:T(128)} %param.13) | copy-start | bytes 100
  21.0 1.1 copy-start.7
  24.4 3.1 %copy-start.11 = (f32[16,32]{1,0:T(8,128)S(1)}, f32[16,32]{1,0:T(8,128)}, u32[]{:S(2)}) copy-start(f32[16,32]{1,0:T(8,128)} %param.10) | copy-start | bytes 6148
  52.5 7.4 %collective-permute-start.2 = (bf16[512,128]{0,1:T(8,128)(2,1)}, bf16[512,128]{0,1:T(8,128)(2,1)}, u32[]{:S(2)}, u32[]{:S(2)}) collective-permute-start(bf16[512,128]{0,1:T(8,128)(2,1)} %collective-permute-done), channel_id=1, source_target_pairs={{0,1},{1,2},{2,3},{3,4},{4,5},{5,6},{6,7},{7,8},{8,9},{9,10},{10,1... | collective-permute-start | bytes 393224 | tf_op jit(solution)/shard_map/ppermute | solution.py:14
  59.9 7.4 %collective-permute-start.4 = (bf16[512,128]{0,1:T(8,128)(2,1)}, bf16[512,128]{0,1:T(8,128)(2,1)}, u32[]{:S(2)}, u32[]{:S(2)}) collective-permute-start(bf16[512,128]{0,1:T(8,128)(2,1)} %collective-permute-done.2), channel_id=1, source_target_pairs={{0,1},{1,2},{2,3},{3,4},{4,5},{5,6},{6,7},{7,8},{8,9},{9,10},{10,1... | collective-permute-start | bytes 393224 | tf_op jit(solution)/shard_map/ppermute | solution.py:14
  84.1 22.4 %collective-permute-start.5 = (f32[16,8]{1,0:T(8,128)}, f32[16,8]{1,0:T(8,128)}, u32[]{:S(2)}, u32[]{:S(2)}) collective-permute-start(f32[16,8]{1,0:T(8,128)} %copy.29), channel_id=1, source_target_pairs={{0,13},{1,14},{2,15},{3,0},{4,1},{5,2},{6,3},{7,4},{8,5},{9,6},{10... | collective-permute-start | bytes 1544 | tf_op jit(solution)/shard_map/ppermute | solution.py:14
  89.8 16.8 %collective-permute-start.1 = (f32[16,8]{1,0:T(8,128)}, f32[16,8]{1,0:T(8,128)}, u32[]{:S(2)}, u32[]{:S(2)}) collective-permute-start(f32[16,8]{1,0:T(8,128)} %copy.27), channel_id=1, source_target_pairs={{0,15},{1,0},{2,1},{3,2},{4,3},{5,4},{6,5},{7,6},{8,7},{9,8},{10,9... | collective-permute-start | bytes 1544 | tf_op jit(solution)/shard_map/ppermute | solution.py:14
  97.4 9.1 %collective-permute-start.3 = (f32[16,8]{1,0:T(8,128)}, f32[16,8]{1,0:T(8,128)}, u32[]{:S(2)}, u32[]{:S(2)}) collective-permute-start(f32[16,8]{1,0:T(8,128)} %copy.28), channel_id=1, source_target_pairs={{0,14},{1,15},{2,0},{3,1},{4,2},{5,3},{6,4},{7,5},{8,6},{9,7},{10,... | collective-permute-start | bytes 1544 | tf_op jit(solution)/shard_map/ppermute | solution.py:14
  109.6 13.0 %collective-permute-start.6 = (f32[16,8]{1,0:T(8,128)}, f32[16,8]{1,0:T(8,128)}, u32[]{:S(2)}, u32[]{:S(2)}) collective-permute-start(f32[16,8]{1,0:T(8,128)} %get-tuple-element.19), channel_id=1, source_target_pairs={{0,1},{1,2},{2,3},{3,4},{4,5},{5,6},{6,7},{7,8},{8,9},{9,10},{10,1... | collective-permute-start | bytes 1544 | tf_op jit(solution)/shard_map/ppermute | solution.py:14
  110.4 20.3 %collective-permute-start.10 = (f32[16,8]{1,0:T(8,128)}, f32[16,8]{1,0:T(8,128)}, u32[]{:S(2)}, u32[]{:S(2)}) collective-permute-start(f32[16,8]{1,0:T(8,128)} %get-tuple-element.17), channel_id=1, source_target_pairs={{0,3},{1,4},{2,5},{3,6},{4,7},{5,8},{6,9},{7,10},{8,11},{9,12},{10... | collective-permute-start | bytes 1544 | tf_op jit(solution)/shard_map/ppermute | solution.py:14
  113.8 13.1 %collective-permute-start.8 = (f32[16,8]{1,0:T(8,128)}, f32[16,8]{1,0:T(8,128)}, u32[]{:S(2)}, u32[]{:S(2)}) collective-permute-start(f32[16,8]{1,0:T(8,128)} %get-tuple-element.18), channel_id=1, source_target_pairs={{0,2},{1,3},{2,4},{3,5},{4,6},{5,7},{6,8},{7,9},{8,10},{9,11},{10,... | collective-permute-start | bytes 1544 | tf_op jit(solution)/shard_map/ppermute | solution.py:14
  141.5 3.1 %copy-start.6 = (f32[512,8]{0,1:T(8,128)S(1)}, f32[512,8]{0,1:T(8,128)}, u32[]{:S(2)}) copy-start(f32[512,8]{0,1:T(8,128)} %div.133) | copy-start | bytes 49156
  146.7 3.1 %copy-start.12 = (pred[1440]{0:T(1024)(128)(4,1)S(1)}, pred[1440]{0:T(1024)(128)(4,1)}, u32[]{:S(2)}) copy-start(pred[1440]{0:T(1024)(128)(4,1)} %lt.42) | copy-start | bytes 4324
  159.7 11.6 %collective-permute-start.9 = (f32[512,128]{0,1:T(8,128)S(1)}, f32[512,128]{0,1:T(8,128)S(1)}, u32[]{:S(2)}, u32[]{:S(2)}) collective-permute-start(f32[512,128]{0,1:T(8,128)S(1)} %fusion.19), channel_id=1, source_target_pairs={{0,14},{1,15},{2,0},{3,1},{4,2},{5,3},{6,4},{7,5},{8,6},{9,7},{10,... | collective-permute-start | bytes 786440 | tf_op jit(solution)/shard_map/ppermute | solution.py:14
  164.5 10.0 %collective-permute-start.7 = (f32[512,128]{0,1:T(8,128)S(1)}, f32[512,128]{0,1:T(8,128)S(1)}, u32[]{:S(2)}, u32[]{:S(2)}) collective-permute-start(f32[512,128]{0,1:T(8,128)S(1)} %fusion.18), channel_id=1, source_target_pairs={{0,15},{1,0},{2,1},{3,2},{4,3},{5,4},{6,5},{7,6},{8,7},{9,8},{10,9... | collective-permute-start | bytes 786440 | tf_op jit(solution)/shard_map/ppermute | solution.py:14
  164.5 12.8 %collective-permute-start.11 = (f32[512,128]{0,1:T(8,128)S(1)}, f32[512,128]{0,1:T(8,128)S(1)}, u32[]{:S(2)}, u32[]{:S(2)}) collective-permute-start(f32[512,128]{0,1:T(8,128)S(1)} %fusion.20), channel_id=1, source_target_pairs={{0,13},{1,14},{2,15},{3,0},{4,1},{5,2},{6,3},{7,4},{8,5},{9,6},{10... | collective-permute-start | bytes 786440 | tf_op jit(solution)/shard_map/ppermute | solution.py:14
  165.0 3.0 %copy-start.2 = (f32[1440,128]{1,0:T(8,128)S(1)}, f32[1440,128]{1,0:T(8,128)}, u32[]{:S(2)}) copy-start(f32[1440,128]{1,0:T(8,128)} %copy-done.1) | copy-start | bytes 2211844
  165.0 3.0 %copy-start.8 = (f32[1440]{0:T(1024)S(1)}, f32[1440]{0:T(1024)}, u32[]{:S(2)}) copy-start(f32[1440]{0:T(1024)} %copy-done.7) | copy-start | bytes 17284
  169.6 7.7 %copy-start.4 = (f32[512,128]{0,1:T(8,128)S(1)}, f32[512,128]{0,1:T(8,128)}, u32[]{:S(2)}) copy-start(f32[512,128]{0,1:T(8,128)} %copy-done.3) | copy-start | bytes 786436
  169.6 7.7 %copy-start.10 = (f32[512]{0:T(512)S(1)}, f32[512]{0:T(512)}, u32[]{:S(2)}) copy-start(f32[512]{0:T(512)} %copy-done.9) | copy-start | bytes 6148
  (3 other events, 2.3 us)
Sparse Core Ops, SparseCore 0:
  179.1 56.0 reduce-scatter.3
where the time goes:
time: 244 us; the launch traced here: 242 us
  local copies, waits for them, and re-layouts  70.7 us (29%)
  waiting for transfers between devices  64.7 us (27%)
  other arithmetic  33.5 us (14%)
  blocking collectives  24.4 us (10%)
  matrix products  21.7 us (9%)
  between operations  14.3 us (6%)
  starting transfers between devices  12.6 us (5%)
    unnamed x2, waiting for transfers between devices  56.2 us
    all_gather x1, blocking collectives, per_device(): stored = lax.all_gather(teacher_rows, 'blk', axis=0, tiled=True)  24.4 us
    mul x8, local copies, waits for them, and re-layouts, score_grads(): natural_power_entries * scale[:, :, None]  20.6 us
    exp x4, local copies, waits for them, and re-layouts, token_terms(): jnp.exp(token_affinity_table / smoothing_heat_factor)  12.6 us
    ppermute x12, starting transfers between devices, shifted(): return lax.ppermute(value, axis, pairs)  12.6 us
    dot_general x4, matrix products, token_terms(): lax.dot_general(query_flat, passage_flat, (((1,), (1,)), ((), ())), prefe...  11.3 us
    div x8, local copies, waits for them, and re-layouts, score_grads(): score_grad[:, None, :] / power_totals_row.reshape(query_matrix, -1, count)  9.58 us
    convert_element_type x1, other arithmetic, score_grads(): (natural_power_entries * scale[:, :, None]).reshape(rows, -1)  8.56 us
  transfers between devices with their start and end apart: 13, of which 6 were waited for; matrix products, arithmetic and copies ran while one was open for 30% of the time, Pallas kernels for 0%

commit v1 on v0

--- a/solution.py
+++ b/solution.py
@@ -6,6 +6,29 @@
 CYCLE = 4
 smoothing_heat_factor = 0.05
 epsilon = 1e-06
+
+
+def in_order(tiles, dim):
+    shape = list(tiles.shape[1:])
+    shape[dim] *= tiles.shape[0]
+    return jnp.moveaxis(tiles, 0, dim).reshape(shape)
+
+
+def collected_by_bits(value, axis):
+    count, index = (lax.axis_size(axis), lax.axis_index(axis))
+    tiles, bit = (value[None], 1)
+    while bit < count:
+        partner_block = lax.ppermute(tiles, axis, [(i, i ^ bit) for i in range(count)])
+        low = index & bit == 0
+        tiles = jnp.concatenate(
+            [jnp.where(low, tiles, partner_block), jnp.where(low, partner_block, tiles)]
+        )
+        bit *= 2
+    return tiles
+
+
+def doubled_up(x, axis, dim):
+    return in_order(collected_by_bits(x, axis), dim)
 
 
 def shifted(value, axis, steps):
@@ -92,7 +115,7 @@
     )
     query_outgoing = query_unit.astype(jnp.bfloat16)
     passage_send = passage_unit.astype(jnp.bfloat16)
-    stored = lax.all_gather(teacher_rows, "blk", axis=0, tiled=True)
+    stored = doubled_up(teacher_rows, "blk", 0)
     teacher = jnp.take(stored, teacher_pos, axis=0)
     score_parts = []
     held = []

time: 244 us -> 231 us (0.947)
  blocking collectives: 24.4 us -> 0 us
  starting transfers between devices: 12.6 us -> 20.9 us
  local copies, waits for them, and re-layouts: 70.7 us -> 67.5 us
  other arithmetic: 33.5 us -> 36.6 us
  waiting for transfers between devices: 64.7 us -> 67.5 us
    all_gather x1 -> x0, blocking collectives: 24.4 us -> none  [per_device(): stored = lax.all_gather(teacher_rows, 'blk', axis=0, tiled=True)]
    ppermute x0 -> x4, starting transfers between devices: none -> 7.95 us  [collected_by_bits(): lax.ppermute(tiles, axis, [(i, i ^ bit) for i in range(count)])]
    ppermute x0 -> x4, waiting for transfers between devices: none -> 3.03 us  [collected_by_bits(): lax.ppermute(tiles, axis, [(i, i ^ bit) for i in range(count)])]
    select_n x0 -> x4, other arithmetic: none -> 3.01 us  [collected_by_bits(): jnp.where(low, tiles, partner_block)]
    concatenate x0 -> x4, other arithmetic: none -> 2.78 us  [collected_by_bits(): jnp.concatenate([jnp.where(low, tiles, partner_block), jnp.where(low, par...]
    unnamed x30 -> x36, local copies, waits for them, and re-layouts: 6.97 us -> 7.04 us
  transfers between devices with their start and end apart: 13 -> 17, of which waited for: 6 -> 8; matrix products, arithmetic and copies ran while one was open for 30% -> 32% of each run, Pallas kernels for 0% -> 0%
where the time goes in v1:
time: 231 us; the launch traced here: 229 us
  local copies, waits for them, and re-layouts  67.5 us (29%)
  waiting for transfers between devices  67.5 us (29%)
  other arithmetic  36.6 us (16%)
  matrix products  21.7 us (9%)
  starting transfers between devices  20.9 us (9%)
  between operations  14.4 us (6%)
    unnamed x2, waiting for transfers between devices  56.2 us
    mul x8, local copies, waits for them, and re-layouts, score_grads(): natural_power_entries * scale[:, :, None]  20.6 us
    ppermute x12, starting transfers between devices, shifted(): return lax.ppermute(value, axis, pairs)  12.9 us
    exp x4, local copies, waits for them, and re-layouts, token_terms(): jnp.exp(token_affinity_table / smoothing_heat_factor)  12.6 us
    dot_general x4, matrix products, token_terms(): lax.dot_general(query_flat, passage_flat, (((1,), (1,)), ((), ())), prefe...  11.3 us
    div x8, local copies, waits for them, and re-layouts, score_grads(): score_grad[:, None, :] / power_totals_row.reshape(query_matrix, -1, count)  9.59 us
    convert_element_type x1, other arithmetic, score_grads(): (natural_power_entries * scale[:, :, None]).reshape(rows, -1)  8.56 us
    ppermute x12, waiting for transfers between devices, shifted(): return lax.ppermute(value, axis, pairs)  8.21 us
  transfers between devices with their start and end apart: 17, of which 8 were waited for; matrix products, arithmetic and copies ran while one was open for 32% of the time, Pallas kernels for 0%

profile of v1, /device:TPU:0, one launch (start us, length us, event | category | flops | bytes accessed | tf_op | source)
XLA Modules:
  0.0 228.6 jit_solution(17508070008169376658)
XLA Ops:
  12.2 3.4 %copy.26 = bf16[8,180,768]{2,1,0:T(8,128)(2,1)} copy(bf16[8,180,768]{2,0,1:T(8,128)(2,1)} %param.8) | data formatting | bytes 4423680 | tf_op args[1]
  15.6 2.6 %reshape.166 = bf16[1440,768]{1,0:T(8,128)(2,1)S(1)} reshape(bf16[8,180,768]{2,1,0:T(8,128)(2,1)} %copy.26) | data formatting | bytes 4423680 | tf_op jit(solution)/shard_map/reshape | solution.py:109
  20.3 2.1 fusion
  22.9 2.6 %collective-permute-start.1 = (f32[2,16,32]{2,1,0:T(8,128)S(1)}, f32[2,16,32]{2,1,0:T(8,128)}, u32[]{:S(2)}, u32[]{:S(2)}) collective-permute-start(f32[2,16,32]{2,1,0:T(8,128)S(1)} %pad_maximum_fusion.3), channel_id=1, source_target_pairs={{0,2},{1,3},{2,0},{3,1},{4,6},{5,7},{6,4},{7,5},{8,10},{9,11},{10,... | collective-permute-start | bytes 12296 | tf_op jit(solution)/shard_map/ppermute | solution.py:21
  35.3 2.8 %collective-permute-start.3 = (f32[8,16,32]{2,1,0:T(8,128)}, f32[8,16,32]{2,1,0:T(8,128)}, u32[]{:S(2)}, u32[]{:S(2)}) collective-permute-start(f32[8,16,32]{2,1,0:T(8,128)} %pad_maximum_fusion.1), channel_id=1, source_target_pairs={{0,8},{1,9},{2,10},{3,11},{4,12},{5,13},{6,14},{7,15},{8,0},{9,1},... | collective-permute-start | bytes 49160 | tf_op jit(solution)/shard_map/ppermute | solution.py:21
  39.5 3.1 %exp.40 = f32[512,8,180]{0,2,1:T(8,128)} reshape(f32[512,1440]{0,1:T(8,128)} %fusion) | data formatting | bytes 5898240 | tf_op jit(solution)/shard_map/exp | solution.py:55
  44.7 3.1 %fusion.1 = f32[512,1440]{0,1:T(8,128)} fusion(bf16[1440,128]{1,0:T(8,128)(2,1)S(1)} %fusion.16, bf16[512,128]{0,1:T(8,128)(2,1)} %collective-permute-done.4), kind=kOutput, calls=%fused_computation.6 | convolution fusion | flops 189480960 | bytes 3448832 | tf_op jit(solution)/shard_map/dot_general | solution.py:47
  47.8 3.1 %exp.42 = f32[512,8,180]{0,2,1:T(8,128)} reshape(f32[512,1440]{0,1:T(8,128)} %fusion.1) | data formatting | bytes 5898240 | tf_op jit(solution)/shard_map/exp | solution.py:55
  52.5 3.1 %fusion.2 = f32[512,1440]{0,1:T(8,128)} fusion(bf16[1440,128]{1,0:T(8,128)(2,1)S(1)} %fusion.16, bf16[512,128]{0,1:T(8,128)(2,1)} %collective-permute-done.6), kind=kOutput, calls=%fused_computation.7 | convolution fusion | flops 189480960 | bytes 3448832 | tf_op jit(solution)/shard_map/dot_general | solution.py:47
  55.6 3.2 %exp.44 = f32[512,8,180]{0,2,1:T(8,128)} reshape(f32[512,1440]{0,1:T(8,128)} %fusion.2) | data formatting | bytes 5898240 | tf_op jit(solution)/shard_map/exp | solution.py:55
  59.5 3.1 %fusion.3 = f32[512,1440]{0,1:T(8,128)} fusion(bf16[1440,128]{1,0:T(8,128)(2,1)S(1)} %fusion.16, bf16[512,128]{0,1:T(8,128)(2,1)} %collective-permute-done.8), kind=kOutput, calls=%fused_computation.8 | convolution fusion | flops 189480960 | bytes 3448832 | tf_op jit(solution)/shard_map/dot_general | solution.py:47
  62.6 3.2 %exp.46 = f32[512,8,180]{0,2,1:T(8,128)} reshape(f32[512,1440]{0,1:T(8,128)} %fusion.3) | data formatting | bytes 5898240 | tf_op jit(solution)/shard_map/exp | solution.py:55
  65.7 5.7 %select_reduce_fusion.3 = (f32[512,8]{0,1:T(8,128)}, f32[512,8]{0,1:T(8,128)S(1)}, f32[512,8]{0,1:T(8,128)S(1)}, f32[512,8]{0,1:T(8,128)S(1)}) fusion(f32[512,8,180]{0,2,1:T(8,128)} %exp.40, pred[8,180]{1,0:T(8,128)(4,1)S(1)} %copy-done.11, f32[512,8,180]{0,2,1:T(8,128)} %exp.42, f32[512,8,180]{0,2,1:T(8,128)} %exp.44, f32[512,8,180]{0,2,1:T(8,128)} %exp.46), kind=kLoop, calls=%fused_computation.12 | loop fusion | flops 5881856 | bytes 11863456 | tf_op jit(solution)/shard_map/reduce_sum | solution.py:57
  80.3 2.5 %collective-permute-start.5 = (f32[16,8]{1,0:T(8,128)}, f32[16,8]{1,0:T(8,128)}, u32[]{:S(2)}, u32[]{:S(2)}) collective-permute-start(f32[16,8]{1,0:T(8,128)} %copy.27), channel_id=1, source_target_pairs={{0,15},{1,0},{2,1},{3,2},{4,3},{5,4},{6,5},{7,6},{8,7},{9,8},{10,9... | collective-permute-start | bytes 1544 | tf_op jit(solution)/shard_map/ppermute | solution.py:37
  97.4 3.1 %collective-permute-start.14 = (f32[16,8]{1,0:T(8,128)}, f32[16,8]{1,0:T(8,128)}, u32[]{:S(2)}, u32[]{:S(2)}) collective-permute-start(f32[16,8]{1,0:T(8,128)} %get-tuple-element.25), channel_id=1, source_target_pairs={{0,3},{1,4},{2,5},{3,6},{4,7},{5,8},{6,9},{7,10},{8,11},{9,12},{10... | collective-permute-start | bytes 1544 | tf_op jit(solution)/shard_map/ppermute | solution.py:37
  106.1 3.1 %mul.115 = f32[512,1440]{0,1:T(8,128)} reshape(f32[512,8,180]{0,2,1:T(8,128)} %mul.114) | data formatting | bytes 5898240 | tf_op jit(solution)/shard_map/mul | solution.py:73
  123.0 3.1 %mul.124 = f32[512,1440]{0,1:T(8,128)} reshape(f32[512,8,180]{0,2,1:T(8,128)} %mul.123) | data formatting | bytes 5898240 | tf_op jit(solution)/shard_map/mul | solution.py:73
  128.1 3.1 %mul.121 = f32[512,1440]{0,1:T(8,128)} reshape(f32[512,8,180]{0,2,1:T(8,128)} %mul.120) | data formatting | bytes 5898240 | tf_op jit(solution)/shard_map/mul | solution.py:73
  133.4 3.1 %mul.118 = f32[512,1440]{0,1:T(8,128)} reshape(f32[512,8,180]{0,2,1:T(8,128)} %mul.117) | data formatting | bytes 5898240 | tf_op jit(solution)/shard_map/mul | solution.py:73
  136.5 8.6 %multiply_convert_fusion = (bf16[512,1440]{0,1:T(8,128)(2,1)S(1)}, bf16[512,1440]{0,1:T(8,128)(2,1)S(1)}, bf16[512,1440]{0,1:T(8,128)(2,1)S(1)}, bf16[512,1440]{0,1:T(8,128)(2,1)S(1)}) fusion(f32[512,1440]{0,1:T(8,128)} %mul.124, f32[512,1440]{0,1:T(8,128)} %fusion.3, pred[1440]{0:T(1024)(128)(4,1)S(1)} %copy-done.15, f32[512,1440]{0,1:T(8,128)} %mul.118, ...), kind=kLoop, calls=%fused_computation.13 | loop fusion | flops 8847360 | bytes 29492640 | tf_op jit(solution)/shard_map/convert_element_type | solution.py:73
  146.3 4.8 %collective-permute-start.13 = (f32[512,128]{0,1:T(8,128)S(1)}, f32[512,128]{0,1:T(8,128)S(1)}, u32[]{:S(2)}, u32[]{:S(2)}) collective-permute-start(f32[512,128]{0,1:T(8,128)S(1)} %fusion.19), channel_id=1, source_target_pairs={{0,14},{1,15},{2,0},{3,1},{4,2},{5,3},{6,4},{7,5},{8,6},{9,7},{10,... | collective-permute-start | bytes 786440 | tf_op jit(solution)/shard_map/ppermute | solution.py:37
  157.8 3.2 %collective-permute-done.11 = f32[512,128]{0,1:T(8,128)S(1)} collective-permute-done((f32[512,128]{0,1:T(8,128)S(1)}, f32[512,128]{0,1:T(8,128)S(1)}, u32[]{:S(2)}, u32[]{:S(2)}) %collective-permute-start.11) | collective-permute-done | bytes 262176 | tf_op jit(solution)/shard_map/ppermute | solution.py:37
  161.1 2.8 %collective-permute-done.15 = f32[512,128]{0,1:T(8,128)S(1)} collective-permute-done((f32[512,128]{0,1:T(8,128)S(1)}, f32[512,128]{0,1:T(8,128)S(1)}, u32[]{:S(2)}, u32[]{:S(2)}) %collective-permute-start.15) | collective-permute-done | bytes 262176 | tf_op jit(solution)/shard_map/ppermute | solution.py:37
  165.6 56.2 %reduce-scatter.4.cloned.1.call-done = f32[48,128]{1,0:T(8,128)} async-done(((f32[768,128]{1,0:T(8,128)}), f32[48,128]{1,0:T(8,128)}) %reduce-scatter.4.cloned.1.call-update) | async-done | bytes 24592
  (135 shorter events, 79.6 us)
Async XLA Ops:
  7.2 214.6 %reduce-scatter.4.cloned.1.call-start = ((), (), s32[]{:S(2)}) async-start(), calls=%async_computation.1 | async-start | bytes 417792
  7.2 15.7 %collective-permute-start = (f32[1,16,32]{2,1,0:T(8,128)}, f32[1,16,32]{2,1,0:T(8,128)S(1)}, u32[]{:S(2)}, u32[]{:S(2)}) collective-permute-start(f32[1,16,32]{2,1,0:T(8,128)} %bitcast.73), channel_id=1, source_target_pairs={{0,1},{1,0},{2,3},{3,2},{4,5},{5,4},{6,7},{7,6},{8,9},{9,8},{10,11... | collective-permute-start | bytes 6152 | tf_op jit(solution)/shard_map/ppermute | solution.py:21
  10.4 34.3 %collective-permute-start.4 = (bf16[512,128]{0,1:T(8,128)(2,1)S(1)}, bf16[512,128]{0,1:T(8,128)(2,1)}, u32[]{:S(2)}, u32[]{:S(2)}) collective-permute-start(bf16[512,128]{0,1:T(8,128)(2,1)S(1)} %fusion.15), channel_id=1, source_target_pairs={{0,1},{1,2},{2,3},{3,4},{4,5},{5,6},{6,7},{7,8},{8,9},{9,10},{10,1... | collective-permute-start | bytes 393224 | tf_op jit(solution)/shard_map/ppermute | solution.py:37
  19.1 3.3 %copy-start.16 = (s32[16]{0:T(128)S(1)}, s32[16]{0:T(128)}, u32[]{:S(2)}) copy-start(s32[16]{0:T(128)} %param.11) | copy-start | bytes 196
  19.1 3.8 %copy-start.14 = (f32[16,32]{1,0:T(8,128)S(1)}, f32[16,32]{1,0:T(8,128)}, u32[]{:S(2)}) copy-start(f32[16,32]{1,0:T(8,128)} %param.10) | copy-start | bytes 6148
  22.9 4.4 %collective-permute-start.1 = (f32[2,16,32]{2,1,0:T(8,128)S(1)}, f32[2,16,32]{2,1,0:T(8,128)}, u32[]{:S(2)}, u32[]{:S(2)}) collective-permute-start(f32[2,16,32]{2,1,0:T(8,128)S(1)} %pad_maximum_fusion.3), channel_id=1, source_target_pairs={{0,2},{1,3},{2,0},{3,1},{4,6},{5,7},{6,4},{7,5},{8,10},{9,11},{10,... | collective-permute-start | bytes 12296 | tf_op jit(solution)/shard_map/ppermute | solution.py:21
  28.1 3.5 %copy-start.7 = (f32[2,16,32]{2,1,0:T(8,128)}, f32[2,16,32]{2,1,0:T(8,128)S(1)}, u32[]{:S(2)}) copy-start(f32[2,16,32]{2,1,0:T(8,128)S(1)} %get-tuple-element.20) | copy-start | bytes 12292
  28.7 4.6 %collective-permute-start.2 = (f32[4,16,32]{2,1,0:T(8,128)}, f32[4,16,32]{2,1,0:T(8,128)}, u32[]{:S(2)}, u32[]{:S(2)}) collective-permute-start(f32[4,16,32]{2,1,0:T(8,128)} %pad_maximum_fusion.2), channel_id=1, source_target_pairs={{0,4},{1,5},{2,6},{3,7},{4,0},{5,1},{6,2},{7,3},{8,12},{9,13},{10,... | collective-permute-start | bytes 24584 | tf_op jit(solution)/shard_map/ppermute | solution.py:21
  35.3 7.9 %collective-permute-start.3 = (f32[8,16,32]{2,1,0:T(8,128)}, f32[8,16,32]{2,1,0:T(8,128)}, u32[]{:S(2)}, u32[]{:S(2)}) collective-permute-start(f32[8,16,32]{2,1,0:T(8,128)} %pad_maximum_fusion.1), channel_id=1, source_target_pairs={{0,8},{1,9},{2,10},{3,11},{4,12},{5,13},{6,14},{7,15},{8,0},{9,1},... | collective-permute-start | bytes 49160 | tf_op jit(solution)/shard_map/ppermute | solution.py:21
  44.7 7.4 %collective-permute-start.6 = (bf16[512,128]{0,1:T(8,128)(2,1)}, bf16[512,128]{0,1:T(8,128)(2,1)}, u32[]{:S(2)}, u32[]{:S(2)}) collective-permute-start(bf16[512,128]{0,1:T(8,128)(2,1)} %collective-permute-done.4), channel_id=1, source_target_pairs={{0,1},{1,2},{2,3},{3,4},{4,5},{5,6},{6,7},{7,8},{8,9},{9,10},{10,1... | collective-permute-start | bytes 393224 | tf_op jit(solution)/shard_map/ppermute | solution.py:37
  52.1 7.4 %collective-permute-start.8 = (bf16[512,128]{0,1:T(8,128)(2,1)}, bf16[512,128]{0,1:T(8,128)(2,1)}, u32[]{:S(2)}, u32[]{:S(2)}) collective-permute-start(bf16[512,128]{0,1:T(8,128)(2,1)} %collective-permute-done.6), channel_id=1, source_target_pairs={{0,1},{1,2},{2,3},{3,4},{4,5},{5,6},{6,7},{7,8},{8,9},{9,10},{10,1... | collective-permute-start | bytes 393224 | tf_op jit(solution)/shard_map/ppermute | solution.py:37
  62.6 3.2 %copy-start.11 = (pred[8,180]{1,0:T(8,128)(4,1)S(1)}, pred[8,180]{1,0:T(8,128)(4,1)}, u32[]{:S(2)}) copy-start(pred[8,180]{1,0:T(8,128)(4,1)} %iota_compare_fusion) | copy-start | bytes 4324
  75.1 18.6 %collective-permute-start.9 = (f32[16,8]{1,0:T(8,128)}, f32[16,8]{1,0:T(8,128)}, u32[]{:S(2)}, u32[]{:S(2)}) collective-permute-start(f32[16,8]{1,0:T(8,128)} %copy.29), channel_id=1, source_target_pairs={{0,13},{1,14},{2,15},{3,0},{4,1},{5,2},{6,3},{7,4},{8,5},{9,6},{10... | collective-permute-start | bytes 1544 | tf_op jit(solution)/shard_map/ppermute | solution.py:37
  80.3 13.4 %collective-permute-start.5 = (f32[16,8]{1,0:T(8,128)}, f32[16,8]{1,0:T(8,128)}, u32[]{:S(2)}, u32[]{:S(2)}) collective-permute-start(f32[16,8]{1,0:T(8,128)} %copy.27), channel_id=1, source_target_pairs={{0,15},{1,0},{2,1},{3,2},{4,3},{5,4},{6,5},{7,6},{8,7},{9,8},{10,9... | collective-permute-start | bytes 1544 | tf_op jit(solution)/shard_map/ppermute | solution.py:37
  85.8 7.9 %collective-permute-start.7 = (f32[16,8]{1,0:T(8,128)}, f32[16,8]{1,0:T(8,128)}, u32[]{:S(2)}, u32[]{:S(2)}) collective-permute-start(f32[16,8]{1,0:T(8,128)} %copy.28), channel_id=1, source_target_pairs={{0,14},{1,15},{2,0},{3,1},{4,2},{5,3},{6,4},{7,5},{8,6},{9,7},{10,... | collective-permute-start | bytes 1544 | tf_op jit(solution)/shard_map/ppermute | solution.py:37
  96.7 12.5 %collective-permute-start.10 = (f32[16,8]{1,0:T(8,128)}, f32[16,8]{1,0:T(8,128)}, u32[]{:S(2)}, u32[]{:S(2)}) collective-permute-start(f32[16,8]{1,0:T(8,128)} %get-tuple-element.27), channel_id=1, source_target_pairs={{0,1},{1,2},{2,3},{3,4},{4,5},{5,6},{6,7},{7,8},{8,9},{9,10},{10,1... | collective-permute-start | bytes 1544 | tf_op jit(solution)/shard_map/ppermute | solution.py:37
  97.4 19.9 %collective-permute-start.14 = (f32[16,8]{1,0:T(8,128)}, f32[16,8]{1,0:T(8,128)}, u32[]{:S(2)}, u32[]{:S(2)}) collective-permute-start(f32[16,8]{1,0:T(8,128)} %get-tuple-element.25), channel_id=1, source_target_pairs={{0,3},{1,4},{2,5},{3,6},{4,7},{5,8},{6,9},{7,10},{8,11},{9,12},{10... | collective-permute-start | bytes 1544 | tf_op jit(solution)/shard_map/ppermute | solution.py:37
  100.5 13.1 %collective-permute-start.12 = (f32[16,8]{1,0:T(8,128)}, f32[16,8]{1,0:T(8,128)}, u32[]{:S(2)}, u32[]{:S(2)}) collective-permute-start(f32[16,8]{1,0:T(8,128)} %get-tuple-element.26), channel_id=1, source_target_pairs={{0,2},{1,3},{2,4},{3,5},{4,6},{5,7},{6,8},{7,9},{8,10},{9,11},{10,... | collective-permute-start | bytes 1544 | tf_op jit(solution)/shard_map/ppermute | solution.py:37
  128.1 3.1 %copy-start.8 = (f32[512,8]{0,1:T(8,128)S(1)}, f32[512,8]{0,1:T(8,128)}, u32[]{:S(2)}) copy-start(f32[512,8]{0,1:T(8,128)} %div.133) | copy-start | bytes 49156
  146.3 11.5 %collective-permute-start.13 = (f32[512,128]{0,1:T(8,128)S(1)}, f32[512,128]{0,1:T(8,128)S(1)}, u32[]{:S(2)}, u32[]{:S(2)}) collective-permute-start(f32[512,128]{0,1:T(8,128)S(1)} %fusion.19), channel_id=1, source_target_pairs={{0,14},{1,15},{2,0},{3,1},{4,2},{5,3},{6,4},{7,5},{8,6},{9,7},{10,... | collective-permute-start | bytes 786440 | tf_op jit(solution)/shard_map/ppermute | solution.py:37
  151.1 10.0 %collective-permute-start.11 = (f32[512,128]{0,1:T(8,128)S(1)}, f32[512,128]{0,1:T(8,128)S(1)}, u32[]{:S(2)}, u32[]{:S(2)}) collective-permute-start(f32[512,128]{0,1:T(8,128)S(1)} %fusion.18), channel_id=1, source_target_pairs={{0,15},{1,0},{2,1},{3,2},{4,3},{5,4},{6,5},{7,6},{8,7},{9,8},{10,9... | collective-permute-start | bytes 786440 | tf_op jit(solution)/shard_map/ppermute | solution.py:37
  151.1 12.8 %collective-permute-start.15 = (f32[512,128]{0,1:T(8,128)S(1)}, f32[512,128]{0,1:T(8,128)S(1)}, u32[]{:S(2)}, u32[]{:S(2)}) collective-permute-start(f32[512,128]{0,1:T(8,128)S(1)} %fusion.20), channel_id=1, source_target_pairs={{0,13},{1,14},{2,15},{3,0},{4,1},{5,2},{6,3},{7,4},{8,5},{9,6},{10... | collective-permute-start | bytes 786440 | tf_op jit(solution)/shard_map/ppermute | solution.py:37
  156.4 7.5 %copy-start.4 = (f32[512,128]{0,1:T(8,128)S(1)}, f32[512,128]{0,1:T(8,128)}, u32[]{:S(2)}) copy-start(f32[512,128]{0,1:T(8,128)} %copy-done.3) | copy-start | bytes 786436
  156.4 7.5 %copy-start.13 = (f32[512]{0:T(512)S(1)}, f32[512]{0:T(512)}, u32[]{:S(2)}) copy-start(f32[512]{0:T(512)} %copy-done.12) | copy-start | bytes 6148
  (10 other events, 16.8 us)
Sparse Core Ops, SparseCore 0:
  165.7 56.0 reduce-scatter.3
